TPU v7x, 128 devices: a whole 4x4x4 slice. The times are simulated.
128 devices in a mesh: row: 16 (over z_hi, y, core), col: 8 (over x, z_lo).
Axes of the slice: x: 4, y: 4, z: 4 (z_hi: 2, z_lo: 2; z = z_hi * 2 + z_lo), core: 2. Of those that a mesh axis runs over, the one named last changes fastest.
Arguments:
- word_topic: bfloat16 [131072, 128], P(('row', 'col')), may hold values from 0.25 to 4
- topic_weight: float32 [128], replicated, may hold values from 0.1 to 10
- tile_blocks: int32 [16, 8, 64, 2], P('row', 'col'), may hold values from 0 to 63, as said below
- tile_live: int32 [16, 8], P('row', 'col'), may hold values from 16 to 64, as said below
- pair_counts: int32 [16, 8, 64, 256, 256], P('row', 'col'), may hold values from 0 to 63
Outputs:
- next_word_topic: bfloat16 [131072, 128], P(('row', 'col'))
- next_topic_weight: float32 [128], replicated
Inputs may be any that keep to these rules, and one draw needn't show every extreme that they name: `tile_blocks`: each entry pair is (a word block among the device's 32 blocks of first words, a word block among its 64 blocks of second words); the slots of one device name distinct tiles. `tile_live`: slots at or beyond a device's count hold no tile; some device fills all slots.
All inputs are finite; a program needn't handle non-finite values.
Results may differ from a plain program's by a relative error of at most 0.0049.
Values may be sent and summed in bfloat16 or wider, within the bound.
No kernel may reach another device: no remote copies, remote signals or barrier semaphores. Data moves between devices by JAX's collectives and lax.ppermute only.
A program may use at most 128 MiB of HBM per device.

v0:
```python
from functools import partial
import jax
import jax.numpy as jnp
from jax import lax
from jax.sharding import PartitionSpec as P

V = 131072
K = 128
BLK = 256
ITERS = 2


def group_step(
    left_blocks, right_blocks, blocks, tiles_all, live, want_row, want_col, group, carry
):
    tile_group = 8
    start = group * tile_group
    row_ids = lax.dynamic_slice_in_dim(blocks[:, 0], start, tile_group)
    col_ids = lax.dynamic_slice_in_dim(blocks[:, 1], start, tile_group)
    tiles = lax.dynamic_slice_in_dim(tiles_all, start, tile_group, 0)
    alive = start + jnp.arange(tile_group, dtype=jnp.int32) < live
    left = left_blocks[row_ids]
    right = right_blocks[col_ids]
    denoms = jnp.einsum("gak,gbk->gab", left, right, preferred_element_type=jnp.float32)
    ratio = jnp.where(alive[:, None, None], tiles.astype(jnp.float32) / denoms, 0.0).astype(
        jnp.bfloat16
    )
    results = []
    place = 0
    row_part = jnp.einsum("gab,gbk->gak", ratio, right, preferred_element_type=jnp.float32)
    results.append(carry[place].at[row_ids].add(row_part))
    place = place + 1
    col_part = jnp.einsum("gab,gak->gbk", ratio, left, preferred_element_type=jnp.float32)
    results.append(carry[place].at[col_ids].add(col_part))
    return tuple(results)


def sweep(left_blocks, right_blocks, blocks, tiles_all, live):
    starts = []
    starts.append(jnp.zeros(left_blocks.shape, jnp.float32))
    starts.append(jnp.zeros(right_blocks.shape, jnp.float32))
    stepper = partial(group_step, left_blocks, right_blocks, blocks, tiles_all, live, True, True)
    turns = (live + 7) // 8
    return lax.fori_loop(0, turns, stepper, tuple(starts))


def local(word_topic, topic_weight, tile_blocks, tile_live, pair_counts):
    blocks = tile_blocks[0, 0]
    live = tile_live[0, 0]
    tiles_all = pair_counts[0, 0]
    weights = word_topic
    shares = topic_weight
    for step in range(ITERS):
        row_phi = lax.all_gather(weights, "col", axis=0, tiled=True)
        col_phi = lax.all_gather(weights, "row", axis=0, tiled=True)
        scaled = (row_phi.astype(jnp.float32) * shares).astype(jnp.bfloat16)
        left_blocks = scaled.reshape(-1, BLK, K)
        right_blocks = col_phi.reshape(-1, BLK, K)
        row_acc, col_acc = sweep(left_blocks, right_blocks, blocks, tiles_all, live)
        row_terms = row_acc.reshape(-1, K)
        col_terms = col_acc.reshape(-1, K)
        row_sum = lax.psum_scatter(row_terms, "col", scatter_dimension=0, tiled=True)
        col_sum = lax.psum_scatter(col_terms, "row", scatter_dimension=0, tiled=True)
        expected = weights.astype(jnp.float32) * (shares * row_sum + col_sum)
        totals = lax.psum(jnp.sum(expected, axis=0), ("row", "col"))
        weights = (V * expected / totals).astype(jnp.bfloat16)
        shares = K * totals / jnp.sum(totals)
    return (weights, shares)


def solution(mesh):
    in_specs = (
        P(("row", "col"), None),
        P(),
        P("row", "col", None, None),
        P("row", "col"),
        P("row", "col", None, None, None),
    )
    out_specs = (P(("row", "col"), None), P())
    return jax.shard_map(local, mesh=mesh, in_specs=in_specs, out_specs=out_specs, check_vma=False)
```

profile of v0, /device:TPU:1, one launch (start us, length us, event | category | flops | bytes accessed | tf_op | source)
XLA Modules:
  0.0 1029.4 jit_solution(16607636807630387287)
XLA Ops:
  9.4 52.8 %all-gather.5.cloned.1.call-done = bf16[8192,128]{1,0:T(8,128)(2,1)} async-done(((bf16[1024,128]{1,0:T(8,128)(2,1)}), bf16[8192,128]{1,0:T(8,128)(2,1)}) %all-gather.5.cloned.1.call-update) | async-done | bytes 2097168 | tf_op jit(solution)/shard_map/all_gather | solution.py:54
  62.1 3.3 multiply_convert_fusion.1
  65.5 57.8 %all-gather.7.cloned.1.call-done = bf16[16384,128]{1,0:T(8,128)(2,1)} async-done(((bf16[1024,128]{1,0:T(8,128)(2,1)}), bf16[16384,128]{1,0:T(8,128)(2,1)}) %all-gather.7.cloned.1.call-update) | async-done | bytes 4194320 | tf_op jit(solution)/shard_map/all_gather | solution.py:55
  123.3 4.2 broadcast.60.clone
  130.0 108.6 %while.24 = (s32[]{:T(128)}, f32[32,256,128]{2,1,0:T(8,128)}, f32[64,256,128]{2,1,0:T(8,128)}, s32[]{:T(128)}, s32[64,2]{0,1:T(2,128)S(1)}, /*index=5*/s32[]{:T(...) while((s32[]{:T(128)}, f32[32,256,128]{2,1,0:T(8,128)}, ...), condition=%wide.region_3.4_spmd, body=%wide.region_0.3_spmd.sunk | while | flops 405276736 | bytes 17835532 | solution.py:44
  138.4 3.4 scatter_fusion.1
  142.3 3.3 scatter_fusion
  154.1 3.3 scatter_fusion.1
  173.3 3.3 scatter_fusion
  185.0 3.4 scatter_fusion.1
  216.0 3.4 scatter_fusion.1
  231.5 3.4 scatter_fusion.1
  235.3 3.4 scatter_fusion
  239.3 103.5 %reduce-scatter.5.cloned.1.call-done = f32[1024,128]{1,0:T(8,128)} async-done(((f32[8192,128]{1,0:T(8,128)}), f32[1024,128]{1,0:T(8,128)}) %reduce-scatter.5.cloned.1.call-update) | async-done | bytes 524304 | tf_op jit(solution)/shard_map/reduce_scatter | solution.py:62
  342.8 106.7 %reduce-scatter.7.cloned.1.call-done = f32[1024,128]{1,0:T(8,128)} async-done(((f32[16384,128]{1,0:T(8,128)}), f32[1024,128]{1,0:T(8,128)}) %reduce-scatter.7.cloned.1.call-update) | async-done | bytes 524304 | tf_op jit(solution)/shard_map/reduce_scatter | solution.py:63
  450.9 65.3 %psum.14 = f32[128]{0:T(128)S(1)} all-reduce(f32[128]{0:T(128)S(1)} %fusion.4), channel_id=1, replica_groups=mesh['row'=16,'col'=8] {'row','col'}, use_global_device_ids=true, to_apply=%region_7.8 | all-reduce | flops 128 | bytes 1024 | tf_op jit(solution)/shard_map/psum | solution.py:65
  520.1 43.9 %all-gather.9.cloned.1.call-done = bf16[8192,128]{1,0:T(8,128)(2,1)} async-done(((bf16[1024,128]{1,0:T(8,128)(2,1)}), bf16[8192,128]{1,0:T(8,128)(2,1)}) %all-gather.9.cloned.1.call-update) | async-done | bytes 2097168 | tf_op jit(solution)/shard_map/all_gather | solution.py:54
  564.1 3.3 multiply_convert_fusion
  567.4 58.3 %all-gather.11.cloned.1.call-done = bf16[16384,128]{1,0:T(8,128)(2,1)} async-done(((bf16[1024,128]{1,0:T(8,128)(2,1)}), bf16[16384,128]{1,0:T(8,128)(2,1)}) %all-gather.11.cloned.1.call-update) | async-done | bytes 4194320 | tf_op jit(solution)/shard_map/all_gather | solution.py:55
  625.7 4.2 broadcast.60
  632.4 108.6 %while.25 = (s32[]{:T(128)}, f32[32,256,128]{2,1,0:T(8,128)}, f32[64,256,128]{2,1,0:T(8,128)}, s32[]{:T(128)}, s32[64,2]{0,1:T(2,128)S(1)}, /*index=5*/s32[]{:T(...) while((s32[]{:T(128)}, f32[32,256,128]{2,1,0:T(8,128)}, ...), condition=%wide.region_12.13_spmd, body=%wide.region_9.12_spmd.sunk | while | flops 405276736 | bytes 17835532 | solution.py:44
  640.8 3.4 scatter_fusion.3
  644.6 3.3 scatter_fusion.2
  656.4 3.3 scatter_fusion.3
  675.6 3.3 scatter_fusion.2
  687.4 3.4 scatter_fusion.3
  718.4 3.4 scatter_fusion.3
  733.9 3.4 scatter_fusion.3
  737.7 3.4 scatter_fusion.2
  741.8 103.4 %reduce-scatter.9.cloned.1.call-done = f32[1024,128]{1,0:T(8,128)} async-done(((f32[8192,128]{1,0:T(8,128)}), f32[1024,128]{1,0:T(8,128)}) %reduce-scatter.9.cloned.1.call-update) | async-done | bytes 524304 | tf_op jit(solution)/shard_map/reduce_scatter | solution.py:62
  845.2 106.7 %reduce-scatter.11.cloned.1.call-done = f32[1024,128]{1,0:T(8,128)} async-done(((f32[16384,128]{1,0:T(8,128)}), f32[1024,128]{1,0:T(8,128)}) %reduce-scatter.11.cloned.1.call-update) | async-done | bytes 524304 | tf_op jit(solution)/shard_map/reduce_scatter | solution.py:63
  953.2 65.5 %psum.15 = f32[128]{0:T(128)S(1)} all-reduce(f32[128]{0:T(128)S(1)} %fusion.5), channel_id=1, replica_groups=mesh['row'=16,'col'=8] {'row','col'}, use_global_device_ids=true, to_apply=%region_16.17 | all-reduce | flops 128 | bytes 1024 | tf_op jit(solution)/shard_map/psum | solution.py:65
  (186 shorter events, 180.9 us)
Async XLA Ops:
  7.2 55.0 %all-gather.5.cloned.1.call-start = ((), (), s32[]{:S(2)}) async-start(), calls=%async_computation.4 | async-start | bytes 2359296 | tf_op jit(solution)/shard_map/all_gather | solution.py:54
  7.9 115.4 %all-gather.7.cloned.1.call-start = ((), (), s32[]{:S(2)}) async-start(), calls=%async_computation.5 | async-start | bytes 4456448 | tf_op jit(solution)/shard_map/all_gather | solution.py:55
  8.6 334.2 %reduce-scatter.5.cloned.1.call-start = ((), (), s32[]{:S(2)}) async-start(), calls=%async_computation.6 | async-start | bytes 4718592 | tf_op jit(solution)/shard_map/reduce_scatter | solution.py:62
  127.6 2.5 copy-start.2
  238.7 210.9 %reduce-scatter.7.cloned.1.call-start = ((), (), s32[]{:S(2)}) async-start(), calls=%async_computation.7 | async-start | bytes 8912896 | tf_op jit(solution)/shard_map/reduce_scatter | solution.py:63
  238.7 210.8 %copy-start.1 = (bf16[1024,128]{1,0:T(8,128)(2,1)S(1)}, bf16[1024,128]{1,0:T(8,128)(2,1)}, u32[]{:S(2)}) copy-start(bf16[1024,128]{1,0:T(8,128)(2,1)} %param.9) | copy-start | bytes 786436
  238.7 210.8 %copy-start.3 = (f32[128]{0:T(128)S(1)}, f32[128]{0:T(128)}, u32[]{:S(2)}) copy-start(f32[128]{0:T(128)} %param.10) | copy-start | bytes 1540
  239.3 324.8 %all-gather.9.cloned.1.call-start = ((), (), s32[]{:S(2)}) async-start(), calls=%async_computation.8 | async-start | bytes 2359296 | tf_op jit(solution)/shard_map/all_gather | solution.py:54
  518.2 107.5 %all-gather.11.cloned.1.call-start = ((), (), s32[]{:S(2)}) async-start(), calls=%async_computation.9 | async-start | bytes 4456448 | tf_op jit(solution)/shard_map/all_gather | solution.py:55
  518.8 326.4 %reduce-scatter.9.cloned.1.call-start = ((), (), s32[]{:S(2)}) async-start(), calls=%async_computation.10 | async-start | bytes 4718592 | tf_op jit(solution)/shard_map/reduce_scatter | solution.py:62
  741.0 210.8 %reduce-scatter.11.cloned.1.call-start = ((), (), s32[]{:S(2)}) async-start(), calls=%async_computation.11 | async-start | bytes 8912896 | tf_op jit(solution)/shard_map/reduce_scatter | solution.py:63
  741.1 210.8 %copy-start = (bf16[1024,128]{1,0:T(8,128)(2,1)S(1)}, bf16[1024,128]{1,0:T(8,128)(2,1)}, u32[]{:S(2)}) copy-start(bf16[1024,128]{1,0:T(8,128)(2,1)} %divide_convert_fusion.1) | copy-start | bytes 786436
Sparse Core Ops, SparseCore 0:
  9.6 52.4 all-gather.4
  64.6 58.7 all-gather.6
  238.8 103.9 reduce-scatter.4
  347.0 102.4 reduce-scatter.6
  518.3 45.6 all-gather.8
  566.9 58.7 all-gather.10
  741.2 103.9 reduce-scatter.8
  849.5 102.2 reduce-scatter.10
where the time goes:
time: 1030 us
  waiting for transfers between devices  636 us (62%)
  blocking collectives  131 us (13%)
  other arithmetic  120 us (12%)
  local copies, waits for them, and re-layouts  84.5 us (8%)
  matrix products  41.8 us (4%)
  between operations  14.8 us (1%)
    reduce_scatter x2, waiting for transfers between devices, local(): lax.psum_scatter(col_terms, 'row', scatter_dimension=0, tiled=True)  213 us
    reduce_scatter x2, waiting for transfers between devices, local(): lax.psum_scatter(row_terms, 'col', scatter_dimension=0, tiled=True)  207 us
    psum x2, blocking collectives, local(): totals = lax.psum(jnp.sum(expected, axis=0), ('row', 'col'))  131 us
    all_gather x2, waiting for transfers between devices, local(): col_phi = lax.all_gather(weights, 'row', axis=0, tiled=True)  116 us
    all_gather x2, waiting for transfers between devices, local(): row_phi = lax.all_gather(weights, 'col', axis=0, tiled=True)  96.7 us
    scatter-add x14, other arithmetic, group_step(): results.append(carry[place].at[col_ids].add(col_part))  46.9 us
    scatter-add x14, other arithmetic, group_step(): results.append(carry[place].at[row_ids].add(row_part))  46.4 us
    gather x14, local copies, waits for them, and re-layouts, group_step(): right = right_blocks[col_ids]  39.7 us
  transfers between devices with their start and end apart: 8, of which 8 were waited for; matrix products, arithmetic and copies ran while one was open for 1% of the time, Pallas kernels for 0%

commit v1 on v0

--- a/solution.py
+++ b/solution.py
@@ -51,7 +51,9 @@
     weights = word_topic
     shares = topic_weight
     for step in range(ITERS):
-        row_phi = lax.all_gather(weights, "col", axis=0, tiled=True)
+        row_phi = jnp.concatenate(
+            lax.all_to_all(jnp.stack([weights] * lax.axis_size("col")), "col", 0, 0), axis=0
+        )
         col_phi = lax.all_gather(weights, "row", axis=0, tiled=True)
         scaled = (row_phi.astype(jnp.float32) * shares).astype(jnp.bfloat16)
         left_blocks = scaled.reshape(-1, BLK, K)

time: 1030 us -> 956 us (0.928)
  waiting for transfers between devices: 636 us -> 547 us
    all_gather x2 -> x0, waiting for transfers between devices: 96.7 us -> none  [local(): row_phi = lax.all_gather(weights, 'col', axis=0, tiled=True)]
    all_to_all x0 -> x2, waiting for transfers between devices: none -> 58.7 us  [local(): lax.all_to_all(jnp.stack([weights] * lax.axis_size('col')), 'col', 0, 0)]
    all_gather x2, waiting for transfers between devices: 116 us -> 66.4 us  [local(): col_phi = lax.all_gather(weights, 'row', axis=0, tiled=True)]
where the time goes in v1:
time: 956 us; the launch traced here: 952 us
  waiting for transfers between devices  547 us (57%)
  blocking collectives  131 us (14%)
  other arithmetic  117 us (12%)
  local copies, waits for them, and re-layouts  89.6 us (9%)
  matrix products  41.8 us (4%)
  between operations  14.8 us (2%)
  starting transfers between devices  10 us (1%)
    reduce_scatter x2, waiting for transfers between devices, local(): lax.psum_scatter(col_terms, 'row', scatter_dimension=0, tiled=True)  213 us
    reduce_scatter x2, waiting for transfers between devices, local(): lax.psum_scatter(row_terms, 'col', scatter_dimension=0, tiled=True)  207 us
    psum x2, blocking collectives, local(): totals = lax.psum(jnp.sum(expected, axis=0), ('row', 'col'))  131 us
    all_gather x2, waiting for transfers between devices, local(): col_phi = lax.all_gather(weights, 'row', axis=0, tiled=True)  66.4 us
    all_to_all x2, waiting for transfers between devices, local(): lax.all_to_all(jnp.stack([weights] * lax.axis_size('col')), 'col', 0, 0)  58.7 us
    scatter-add x14, other arithmetic, group_step(): results.append(carry[place].at[col_ids].add(col_part))  46.9 us
    scatter-add x14, other arithmetic, group_step(): results.append(carry[place].at[row_ids].add(row_part))  46.4 us
    gather x14, local copies, waits for them, and re-layouts, group_step(): right = right_blocks[col_ids]  39.7 us
  transfers between devices with their start and end apart: 8, of which 8 were waited for; matrix products, arithmetic and copies ran while one was open for 1% of the time, Pallas kernels for 0%

profile of v1, /device:TPU:1, one launch (start us, length us, event | category | flops | bytes accessed | tf_op | source)
XLA Modules:
  0.0 952.4 jit_solution(12244980892089200705)
XLA Ops:
  10.5 6.2 all-to-all-start
  17.4 29.8 %all-to-all-done = bf16[8,1024,128]{2,1,0:T(8,128)(2,1)S(1)} async-done(((bf16[8,1024,128]{2,1,0:T(8,128)(2,1)}), bf16[8,1024,128]{2,1,0:T(8,128)(2,1)S(1)}, u32[]{:S(2)}, u32[]{:S(2)}) %all-to-all-start) | async-done | bytes 2097184 | tf_op jit(solution)/shard_map/all_to_all | solution.py:55
  49.1 34.6 %all-gather.3.cloned.1.call-done = bf16[16384,128]{1,0:T(8,128)(2,1)} async-done(((bf16[1024,128]{1,0:T(8,128)(2,1)}), bf16[16384,128]{1,0:T(8,128)(2,1)}) %all-gather.3.cloned.1.call-update) | async-done | bytes 4194320 | tf_op jit(solution)/shard_map/all_gather | solution.py:57
  83.7 4.2 broadcast.74.clone
  90.4 108.6 %while.24 = (s32[]{:T(128)}, f32[32,256,128]{2,1,0:T(8,128)}, f32[64,256,128]{2,1,0:T(8,128)}, s32[]{:T(128)}, s32[64,2]{0,1:T(2,128)S(1)}, /*index=5*/s32[]{:T(...) while((s32[]{:T(128)}, f32[32,256,128]{2,1,0:T(8,128)}, ...), condition=%wide.region_3.4_spmd, body=%wide.region_0.3_spmd.sunk | while | flops 405276736 | bytes 17835532 | solution.py:44
  98.8 3.4 scatter_fusion.1
  102.7 3.3 scatter_fusion
  114.5 3.3 scatter_fusion.1
  133.7 3.3 scatter_fusion
  145.4 3.4 scatter_fusion.1
  176.4 3.4 scatter_fusion.1
  191.9 3.4 scatter_fusion.1
  195.7 3.4 scatter_fusion
  199.9 103.4 %reduce-scatter.5.cloned.1.call-done = f32[1024,128]{1,0:T(8,128)} async-done(((f32[8192,128]{1,0:T(8,128)}), f32[1024,128]{1,0:T(8,128)}) %reduce-scatter.5.cloned.1.call-update) | async-done | bytes 524304 | tf_op jit(solution)/shard_map/reduce_scatter | solution.py:64
  303.2 106.7 %reduce-scatter.7.cloned.1.call-done = f32[1024,128]{1,0:T(8,128)} async-done(((f32[16384,128]{1,0:T(8,128)}), f32[1024,128]{1,0:T(8,128)}) %reduce-scatter.7.cloned.1.call-update) | async-done | bytes 524304 | tf_op jit(solution)/shard_map/reduce_scatter | solution.py:65
  411.3 65.5 %psum.14 = f32[128]{0:T(128)S(1)} all-reduce(f32[128]{0:T(128)S(1)} %fusion.6), channel_id=1, replica_groups=mesh['row'=16,'col'=8] {'row','col'}, use_global_device_ids=true, to_apply=%region_7.8 | all-reduce | flops 128 | bytes 1024 | tf_op jit(solution)/shard_map/psum | solution.py:67
  481.4 3.6 all-to-all-start.1
  486.3 28.9 %all-to-all-done.1 = bf16[8,1024,128]{2,1,0:T(8,128)(2,1)S(1)} async-done(((bf16[8,1024,128]{2,1,0:T(8,128)(2,1)}), bf16[8,1024,128]{2,1,0:T(8,128)(2,1)S(1)}, u32[]{:S(2)}, u32[]{:S(2)}) %all-to-all-start.1) | async-done | bytes 2097184 | tf_op jit(solution)/shard_map/all_to_all | solution.py:55
  517.1 31.8 %all-gather.5.cloned.1.call-done = bf16[16384,128]{1,0:T(8,128)(2,1)} async-done(((bf16[1024,128]{1,0:T(8,128)(2,1)}), bf16[16384,128]{1,0:T(8,128)(2,1)}) %all-gather.5.cloned.1.call-update) | async-done | bytes 4194320 | tf_op jit(solution)/shard_map/all_gather | solution.py:57
  548.9 4.2 broadcast.74
  555.6 108.6 %while.25 = (s32[]{:T(128)}, f32[32,256,128]{2,1,0:T(8,128)}, f32[64,256,128]{2,1,0:T(8,128)}, s32[]{:T(128)}, s32[64,2]{0,1:T(2,128)S(1)}, /*index=5*/s32[]{:T(...) while((s32[]{:T(128)}, f32[32,256,128]{2,1,0:T(8,128)}, ...), condition=%wide.region_12.13_spmd, body=%wide.region_9.12_spmd.sunk | while | flops 405276736 | bytes 17835532 | solution.py:44
  564.0 3.4 scatter_fusion.3
  567.9 3.3 scatter_fusion.2
  579.6 3.3 scatter_fusion.3
  598.9 3.3 scatter_fusion.2
  610.6 3.4 scatter_fusion.3
  641.6 3.4 scatter_fusion.3
  657.1 3.4 scatter_fusion.3
  660.9 3.4 scatter_fusion.2
  664.8 103.6 %reduce-scatter.9.cloned.1.call-done = f32[1024,128]{1,0:T(8,128)} async-done(((f32[8192,128]{1,0:T(8,128)}), f32[1024,128]{1,0:T(8,128)}) %reduce-scatter.9.cloned.1.call-update) | async-done | bytes 524304 | tf_op jit(solution)/shard_map/reduce_scatter | solution.py:64
  768.4 106.7 %reduce-scatter.11.cloned.1.call-done = f32[1024,128]{1,0:T(8,128)} async-done(((f32[16384,128]{1,0:T(8,128)}), f32[1024,128]{1,0:T(8,128)}) %reduce-scatter.11.cloned.1.call-update) | async-done | bytes 524304 | tf_op jit(solution)/shard_map/reduce_scatter | solution.py:65
  876.5 65.3 %psum.15 = f32[128]{0:T(128)S(1)} all-reduce(f32[128]{0:T(128)S(1)} %fusion.7), channel_id=1, replica_groups=mesh['row'=16,'col'=8] {'row','col'}, use_global_device_ids=true, to_apply=%region_16.17 | all-reduce | flops 128 | bytes 1024 | tf_op jit(solution)/shard_map/psum | solution.py:67
  (186 shorter events, 188.5 us)
Async XLA Ops:
  7.2 40.0 %copy-start.3 = (f32[128]{0:T(128)S(1)}, f32[128]{0:T(128)}, u32[]{:S(2)}) copy-start(f32[128]{0:T(128)} %param.10) | copy-start | bytes 1540
  7.2 76.5 %all-gather.3.cloned.1.call-start = ((), (), s32[]{:S(2)}) async-start(), calls=%async_computation.6 | async-start | bytes 4456448 | tf_op jit(solution)/shard_map/all_gather | solution.py:57
  10.5 36.7 %all-to-all-start = ((bf16[8,1024,128]{2,1,0:T(8,128)(2,1)}), bf16[8,1024,128]{2,1,0:T(8,128)(2,1)S(1)}, u32[]{:S(2)}, u32[]{:S(2)}) async-start(bf16[8,1024,128]{2,1,0:T(8,128)(2,1)} %stack.4), calls=%async_computation | async-start | bytes 4194304 | tf_op jit(solution)/shard_map/all_to_all | solution.py:55
  16.7 286.5 %reduce-scatter.5.cloned.1.call-start = ((), (), s32[]{:S(2)}) async-start(), calls=%async_computation.7 | async-start | bytes 4718592 | tf_op jit(solution)/shard_map/reduce_scatter | solution.py:64
  88.0 2.5 copy-start.2
  199.1 210.8 %reduce-scatter.7.cloned.1.call-start = ((), (), s32[]{:S(2)}) async-start(), calls=%async_computation.8 | async-start | bytes 8912896 | tf_op jit(solution)/shard_map/reduce_scatter | solution.py:65
  199.1 210.8 %copy-start.1 = (bf16[1024,128]{1,0:T(8,128)(2,1)S(1)}, bf16[1024,128]{1,0:T(8,128)(2,1)}, u32[]{:S(2)}) copy-start(bf16[1024,128]{1,0:T(8,128)(2,1)} %param.9) | copy-start | bytes 786436
  199.8 349.1 %all-gather.5.cloned.1.call-start = ((), (), s32[]{:S(2)}) async-start(), calls=%async_computation.9 | async-start | bytes 4456448 | tf_op jit(solution)/shard_map/all_gather | solution.py:57
  481.4 33.8 %all-to-all-start.1 = ((bf16[8,1024,128]{2,1,0:T(8,128)(2,1)}), bf16[8,1024,128]{2,1,0:T(8,128)(2,1)S(1)}, u32[]{:S(2)}, u32[]{:S(2)}) async-start(bf16[8,1024,128]{2,1,0:T(8,128)(2,1)} %stack.5), calls=%async_computation.3 | async-start | bytes 4194304 | tf_op jit(solution)/shard_map/all_to_all | solution.py:55
  485.0 283.4 %reduce-scatter.9.cloned.1.call-start = ((), (), s32[]{:S(2)}) async-start(), calls=%async_computation.10 | async-start | bytes 4718592 | tf_op jit(solution)/shard_map/reduce_scatter | solution.py:64
  664.3 210.9 %reduce-scatter.11.cloned.1.call-start = ((), (), s32[]{:S(2)}) async-start(), calls=%async_computation.11 | async-start | bytes 8912896 | tf_op jit(solution)/shard_map/reduce_scatter | solution.py:65
  664.3 210.8 %copy-start = (bf16[1024,128]{1,0:T(8,128)(2,1)S(1)}, bf16[1024,128]{1,0:T(8,128)(2,1)}, u32[]{:S(2)}) copy-start(bf16[1024,128]{1,0:T(8,128)(2,1)} %divide_convert_fusion.1) | copy-start | bytes 786436
Sparse Core Ops, SparseCore 0:
  10.4 73.2 all-gather.2
  199.2 103.9 reduce-scatter.4
  307.6 102.2 reduce-scatter.6
  478.9 69.9 all-gather.4
  664.4 103.9 reduce-scatter.8
  772.6 102.5 reduce-scatter.10
